TPU v7x, 128 devices: a whole 4x4x4 slice. The times are simulated.
128 devices in a mesh: replica: 16 (over y_lo, z, core), tensor: 8 (over y_hi, x).
Axes of the slice: x: 4, y: 4 (y_hi: 2, y_lo: 2; y = y_hi * 2 + y_lo), z: 4, core: 2. Of those that a mesh axis runs over, the one named last changes fastest.
Arguments:
- hidden: bfloat16 [128, 2, 8192], P('replica'), may hold values from -6 to 6
- shard_rows: float32 [8704, 18432], P(('replica', 'tensor')), may hold values from -0.0625 to 0.0625
- piece_length: int32 [128], replicated, may hold values from 1 to 68, 8192 in all
- cache_keys: bfloat16 [128, 8, 4096, 128], P('replica', 'tensor'), may hold values from -200 to 200
- cache_values: bfloat16 [128, 8, 4096, 128], P('replica', 'tensor'), may hold values from -6 to 6
- cache_fill: int32 [128], P('replica'), may hold values from 1 to 4096, as said below
Outputs:
- layer_out: bfloat16 [128, 2, 8192], P('replica', None, 'tensor')
Inputs may be any that keep to these rules, and one draw needn't show every extreme that they name: `piece_length`: the device with replica index r and tensor index t holds piece r times the tensor axis size plus t; some piece has exactly 68 rows. `cache_fill`: some row has a full cache.
All inputs are finite; a program needn't handle non-finite values.
Results may differ from a plain program's by a relative error of at most 0.014.
Values may be sent and summed in bfloat16 or wider, within the bound.
No kernel may reach another device: no remote copies, remote signals or barrier semaphores. Data moves between devices by JAX's collectives and lax.ppermute only.
A program may use at most 192 MiB of HBM per device.

v0:
```python
import math
import jax
import jax.numpy as jnp
from jax import lax
from jax.sharding import PartitionSpec as P

D = 8192
HQ = 64
KV = 8
HD = 128
ROPE_BASE = 1000000.0
NEG_FILL = -1e30


def rotate(source, position):
    halfway = source.shape[-1] // 2
    exponent = jnp.arange(halfway, dtype=jnp.float32) * (2.0 / source.shape[-1])
    frequency = jnp.exp(-exponent * math.log(ROPE_BASE))
    angles = position[:, None, None] * frequency[None, None, :]
    cosine = jnp.cos(angles)
    sine_part = jnp.sin(angles)
    former = source[..., :halfway]
    latter = source[..., halfway:]
    return jnp.concatenate(
        [former * cosine - latter * sine_part, latter * cosine + former * sine_part], axis=-1
    )


def attend(projected, keys_cache, values_cache, filled):
    batch_rows, heads_kv, span_len, head_size = keys_cache.shape
    count = projected.shape[0]
    width_kv = heads_kv * head_size
    width_q = projected.shape[1] - 2 * width_kv
    heads_q = width_q // head_size
    group_size = heads_q // heads_kv
    position = (
        (filled[:, None] + jnp.arange(2, dtype=jnp.int32)[None, :]).reshape(-1).astype(jnp.float32)
    )
    query = rotate(projected[:, :width_q].reshape(count, heads_q, head_size), position).astype(
        jnp.bfloat16
    )
    new_key = rotate(
        projected[:, width_q : width_q + width_kv].reshape(count, heads_kv, head_size), position
    ).astype(jnp.bfloat16)
    new_value = (
        projected[:, width_q + width_kv :]
        .astype(jnp.bfloat16)
        .reshape(batch_rows, 2, heads_kv, head_size)
    )
    query = query.reshape(batch_rows, 2, heads_kv, group_size, head_size)
    new_key = new_key.reshape(batch_rows, 2, heads_kv, head_size)
    factor = 1.0 / math.sqrt(head_size)
    cached = (
        jnp.einsum("bskgd,bkcd->bkgsc", query, keys_cache, preferred_element_type=jnp.float32)
        * factor
    )
    recent = (
        jnp.einsum("bskgd,btkd->bkgst", query, new_key, preferred_element_type=jnp.float32) * factor
    )
    visible = (jnp.arange(span_len)[None, :] < filled[:, None])[:, None, None, None, :]
    causal = jnp.arange(2)[:, None] >= jnp.arange(2)[None, :]
    cached = jnp.where(visible, cached, NEG_FILL)
    recent = jnp.where(causal, recent, NEG_FILL)
    highest = jnp.maximum(jnp.max(cached, axis=-1), jnp.max(recent, axis=-1))
    cached_exp = jnp.exp(cached - highest[..., None])
    recent_exp = jnp.exp(recent - highest[..., None])
    total = jnp.sum(cached_exp, axis=-1) + jnp.sum(recent_exp, axis=-1)
    cached_prob = (cached_exp / total[..., None]).astype(jnp.bfloat16)
    recent_prob = (recent_exp / total[..., None]).astype(jnp.bfloat16)
    mixed = jnp.einsum(
        "bkgsc,bkcd->bskgd", cached_prob, values_cache, preferred_element_type=jnp.float32
    )
    mixed = mixed + jnp.einsum(
        "bkgst,btkd->bskgd", recent_prob, new_value, preferred_element_type=jnp.float32
    )
    return mixed.astype(jnp.bfloat16).reshape(count, width_q)


def split_slices(block, slices, width_q, width_kv):
    height = block.shape[0]
    bounds = (0, width_q, width_q + width_kv, width_q + 2 * width_kv, block.shape[1])
    pieces = [
        block[:, bounds[index] : bounds[index + 1]].reshape(height, slices, -1)
        for index in range(4)
    ]
    return jnp.concatenate(pieces, axis=2).astype(jnp.bfloat16)


def padded_columns(matrix, piece_length, starts, capacity):
    offsets = jnp.arange(capacity, dtype=jnp.int32)
    source = (starts[:, None] + offsets[None, :]).reshape(-1)
    valid = (offsets[None, :] < piece_length[:, None]).reshape(-1)
    source = jnp.clip(source, 0, matrix.shape[1] - 1)
    picked = jnp.take(matrix, source, axis=1)
    return jnp.where(valid[None, :], picked, jnp.zeros((), matrix.dtype))


def model_order(padded, piece_ends, starts, capacity):
    global_row = jnp.arange(D, dtype=jnp.int32)
    passed = piece_ends[None, :] <= global_row[:, None]
    owners = jnp.sum(passed.astype(jnp.int32), axis=1)
    own_start = jnp.max(
        jnp.where(starts[None, :] <= global_row[:, None], starts[None, :], 0), axis=1
    )
    source = owners * capacity + (global_row - own_start)
    return jnp.take(padded, source, axis=1)


def body(hidden, shard_rows, piece_length, cache_keys, cache_values, cache_fill):
    slices = lax.axis_size("tensor")
    capacity = shard_rows.shape[0]
    batch_rows = cache_keys.shape[0]
    project_width = (HQ + 2 * KV) * HD // slices
    tokens = hidden.reshape(batch_rows * 2, hidden.shape[2])
    stacked = split_slices(shard_rows, slices, HQ * HD, KV * HD)
    received = lax.all_to_all(stacked, "tensor", split_axis=1, concat_axis=0, tiled=True).reshape(
        slices * capacity, -1
    )
    piece_ends = jnp.cumsum(piece_length)
    starts = piece_ends - piece_length
    gathered = lax.all_gather(received, "replica", axis=0, tiled=True)
    token_cols = padded_columns(tokens, piece_length, starts, capacity)
    projected = jnp.dot(token_cols, gathered[:, :project_width], preferred_element_type=jnp.float32)
    attended = attend(projected, cache_keys, cache_values, cache_fill)
    padded_out = jnp.einsum(
        "tf,jf->tj", attended, gathered[:, project_width:], preferred_element_type=jnp.float32
    )
    partial_value = model_order(padded_out, piece_ends, starts, capacity)
    result = lax.psum_scatter(
        partial_value.astype(jnp.bfloat16), "tensor", scatter_dimension=1, tiled=True
    )
    return result.reshape(batch_rows, 2, -1)


def solution(mesh):
    placed = (
        P("replica", None, None),
        P(("replica", "tensor"), None),
        P(),
        P("replica", "tensor", None, None),
        P("replica", "tensor", None, None),
        P("replica"),
    )
    return jax.shard_map(
        body, mesh=mesh, in_specs=placed, out_specs=P("replica", None, "tensor"), check_vma=False
    )
```

profile of v0, /device:TPU:0, one launch (start us, length us, event | category | flops | bytes accessed | tf_op | source)
XLA Modules:
  0.0 404.8 jit_solution(11453051769635122451)
XLA Ops:
  6.5 0.0 all-gather.2.cloned.1.call-start
  6.5 2.8 convert.33
  9.3 0.2 fusion.56
  9.5 0.7 copy.32
  10.2 0.1 slice.74
  10.3 0.6 copy.21
  10.9 0.7 copy.35
  11.6 0.1 slice.77
  11.7 0.6 copy.24
  12.5 0.2 pad_maximum_fusion
  12.7 41.8 %all_to_all.15 = bf16[68,8,2304]{2,0,1:T(8,128)(2,1)S(1)} all-to-all(bf16[68,8,2304]{2,0,1:T(8,128)(2,1)S(1)} %pad_maximum_fusion), channel_id=1, replica_groups=mesh['replica'=16,'tensor'=8] {'tensor'}, dimensions={1} | all-to-all | bytes 5013504 | tf_op jit(solution)/shard_map/all_to_all | solution.py:116
  54.5 2.2 reshape.409
  56.8 0.0 copy-start.1
  56.8 0.0 copy-start
  56.8 0.0 all-gather.2.cloned.1.call-update
  56.8 0.0 copy-start.2
  56.8 0.0 reduce-scatter.2.cloned.1.call-start
  56.9 0.6 copy-done.1
  57.4 0.1 copy.19
  57.5 0.2 reduce-window.8
  57.7 0.1 reduce.4
  57.8 0.1 add_clamp_fusion
  57.9 0.1 min.18
  58.1 0.1 min.16
  58.2 0.0 copy-done
  58.2 0.1 reshape.404
  58.3 1.0 copy.20
  59.3 0.1 iota_compare_fusion.3
  59.4 0.1 lt.85
  59.5 0.0 copy-done.2
  59.5 0.1 add_convert_fusion.1
  59.6 0.1 convert_element_type.44
  59.7 0.1 fusion.36
  59.8 18.3 %gather_fusion = bf16[8704,16]{1,0:T(8,128)(2,1)} fusion(bf16[16,8192]{0,1:T(8,128)(2,1)S(1)} %copy.20, s32[9216]{0:T(1024)S(1)} %pad_clamp_fusion), kind=kCustom, calls=%fused_computation | custom fusion | bytes 591872 | tf_op jit(solution)/shard_map/jit(_take)/gather | solution.py:94
  78.2 0.1 multiply_cosine_fusion.1
  78.3 2.2 select_reduce_fusion
  80.5 0.1 compare_select_fusion.1
  80.7 0.1 iota_compare_fusion.2
  80.8 175.7 %all-gather.2.cloned.1.call-done = bf16[8704,2304]{1,0:T(8,128)(2,1)} async-done(((bf16[544,2304]{1,0:T(8,128)(2,1)}), bf16[8704,2304]{1,0:T(8,128)(2,1)}) %all-gather.2.cloned.1.call-update) | async-done | bytes 40108048 | tf_op jit(solution)/shard_map/all_gather | solution.py:121
  256.5 10.1 %fusion = f32[16,1280]{1,0:T(8,128)S(1)} fusion(bf16[8704,2304]{1,0:T(8,128)(2,1)} %all-gather.2.cloned.1.call-done, bf16[8704,16]{1,0:T(8,128)(2,1)} %gather_fusion, pred[8704]{0:T(1024)(128)(4,1)S(1)} %lt.85, pred[8704]{0:T(1024)(128)(4,1)S(1)} %compare_and_fusion), kind=kOutput, calls=%fused_computation.2 | convolution fusion | flops 356794368 | bytes 24609792 | tf_op jit(solution)/shard_map/dot_general | solution.py:123
  266.6 0.1 fusion.45
  266.8 0.1 subtract_convert_fusion
  266.9 5.8 %fusion.58 = (f32[8,8,2]{1,2,0:T(2,128)S(1)}, f32[8,1,8,2,4096]{4,2,3,0,1:T(8,128)S(1)}) fusion(bf16[8,1,4096,128]{3,2,1,0:T(8,128)(2,1)} %param.9, bf16[8,2,8,64]{3,2,1,0:T(8,128)(2,1)S(1)} %bitcast.115, bf16[8,2,8,64]{3,2,1,0:T(8,128)(2,1)S(1)} %bitcast.113, pred[8,4096]{1,0:T(8,128)(4,1)S(1)} %iota_compare_fusion.2), kind=kOutput, calls=%fused_computation.88 | convolution fusion | flops 135856000 | bytes 10551808 | tf_op jit(solution)/shard_map/bskgd,bkcd->bkgsc/dot_general | solution.py:54
  272.7 0.4 fusion.59
  273.1 0.4 fusion.25
  273.5 4.7 %fusion.26 = f32[8,128,8,2]{1,2,3,0:T(8,128)S(1)} fusion(bf16[8,1,4096,128]{3,2,1,0:T(8,128)(2,1)} %param.10, f32[8,1,8,2,4096]{4,2,3,0,1:T(8,128)S(1)} %get-tuple-element.16, f32[8,8,2]{1,2,0:T(2,128)S(1)} %add.134, f32[8,8,2]{1,2,0:T(2,128)S(1)} %max.22), kind=kOutput, calls=%fused_computation.28 | convolution fusion | flops 135790592 | bytes 10552320 | tf_op jit(solution)/shard_map/bkgsc,bkcd->bskgd/dot_general | solution.py:70
  278.2 0.2 fusion.29
  278.5 12.5 %fusion.2 = bf16[16,8704]{0,1:T(8,128)(2,1)} fusion(bf16[8704,2304]{1,0:T(8,128)(2,1)} %all-gather.2.cloned.1.call-done, bf16[2,8,8,128]{3,2,1,0:T(8,128)(2,1)S(1)} %bitcast.123), kind=kOutput, calls=%fused_computation.4 | convolution fusion | flops 285212672 | bytes 18137088 | tf_op jit(solution)/shard_map/tf,jf->tj/dot_general | solution.py:125
  291.0 23.8 %gather_fusion.1 = bf16[8192,16]{1,0:T(8,128)(2,1)S(1)} fusion(bf16[16,8704]{0,1:T(8,128)(2,1)} %fusion.2, s32[8192]{0:T(1024)S(1)} %broadcast_clamp_fusion), kind=kCustom, calls=%fused_computation.1 | custom fusion | bytes 557056 | tf_op jit(solution)/shard_map/jit(_take)/gather | solution.py:106
  314.8 5.0 %fusion.24 = bf16[16,8192]{0,1:T(8,128)(2,1)} fusion(bf16[8192,16]{1,0:T(8,128)(2,1)S(1)} %gather_fusion.1, pred[8192]{0:T(1024)(128)(4,1)S(1)} %compare_and_fusion.1), kind=kLoop, calls=%fused_computation.24 | loop fusion | flops 131072 | bytes 532480 | tf_op jit(solution)/shard_map/convert_element_type | solution.py:130
  319.9 0.0 reduce-scatter.2.cloned.1.call-update
  319.9 76.4 %reduce-scatter.2.cloned.1.call-done = bf16[16,1024]{0,1:T(8,128)(2,1)} async-done(((bf16[16,8192]{0,1:T(8,128)(2,1)}), bf16[16,1024]{0,1:T(8,128)(2,1)}) %reduce-scatter.2.cloned.1.call-update) | async-done | bytes 32784 | tf_op jit(solution)/shard_map/reduce_scatter | solution.py:129
  396.3 1.0 copy.26
  397.3 0.6 reshape.418
  (22 shorter events, 0.3 us)
Async XLA Ops:
  6.5 250.0 %all-gather.2.cloned.1.call-start = ((), (), s32[]{:S(2)}) async-start(), calls=%async_computation.2 | async-start | bytes 42614784 | tf_op jit(solution)/shard_map/all_gather | solution.py:121
  56.8 0.7 copy-start.1
  56.8 1.4 copy-start
  56.8 2.7 copy-start.2
  56.8 339.5 %reduce-scatter.2.cloned.1.call-start = ((), (), s32[]{:S(2)}) async-start(), calls=%async_computation.3 | async-start | bytes 2359296 | tf_op jit(solution)/shard_map/reduce_scatter | solution.py:129
Sparse Core Ops, SparseCore 0:
  56.9 199.5 all-gather.1
  320.0 76.2 reduce-scatter.1
where the time goes:
time: 405 us
  waiting for transfers between devices  252 us (62%)
  local copies, waits for them, and re-layouts  51.4 us (13%)
  blocking collectives  41.8 us (10%)
  matrix products  33.7 us (8%)
  between operations  13.8 us (3%)
  other arithmetic  12 us (3%)
    all_gather x1, waiting for transfers between devices, body(): gathered = lax.all_gather(received, 'replica', axis=0, tiled=True)  176 us
    reduce_scatter x1, waiting for transfers between devices, body(): lax.psum_scatter(partial_value.astype(jnp.bfloat16), 'tensor', scatter_di...  76.4 us
    all_to_all x1, blocking collectives, body(): lax.all_to_all(stacked, 'tensor', split_axis=1, concat_axis=0, tiled=True)  41.8 us
    gather x1, local copies, waits for them, and re-layouts, model_order(): return jnp.take(padded, source, axis=1)  23.8 us
    gather x1, local copies, waits for them, and re-layouts, padded_columns(): picked = jnp.take(matrix, source, axis=1)  18.3 us
    dot_general x1, matrix products, body(): jnp.einsum('tf,jf->tj', attended, gathered[:, project_width:], preferred_...  12.5 us
    dot_general x1, matrix products, body(): jnp.dot(token_cols, gathered[:, :project_width], preferred_element_type=j...  10.1 us
  transfers between devices with their start and end apart: 2, of which 2 were waited for; matrix products, arithmetic and copies ran while one was open for 6% of the time, Pallas kernels for 0%

commit v1 on v0

--- a/solution.py
+++ b/solution.py
@@ -118,7 +118,16 @@
     )
     piece_ends = jnp.cumsum(piece_length)
     starts = piece_ends - piece_length
-    gathered = lax.all_gather(received, "replica", axis=0, tiled=True)
+
+    def terms_state(a0, a_name):
+        frames = []
+        for _ in range(lax.psum(1, a_name)):
+            frames.append(a0)
+        return jnp.concatenate(
+            lax.all_to_all(jnp.stack(frames, 0), axis_name=a_name, split_axis=0, concat_axis=0), 0
+        )
+
+    gathered = terms_state(received, "replica")
     token_cols = padded_columns(tokens, piece_length, starts, capacity)
     projected = jnp.dot(token_cols, gathered[:, :project_width], preferred_element_type=jnp.float32)
     attended = attend(projected, cache_keys, cache_values, cache_fill)

time: 405 us -> 850 us (2.10)
  waiting for transfers between devices: 252 us -> 678 us
  local copies, waits for them, and re-layouts: 51.4 us -> 64.9 us
    all_to_all x0 -> x1, waiting for transfers between devices: none -> 605 us  [terms_state(): lax.all_to_all(jnp.stack(frames, 0), axis_name=a_name, split_axis=0, conc...]
    all_gather x1 -> x0, waiting for transfers between devices: 176 us -> none  [body(): gathered = lax.all_gather(received, 'replica', axis=0, tiled=True)]
    another operation x1 -> x3, local copies, waits for them, and re-layouts: 0.11 us -> 16.5 us  [the longest x2 16.4 us: terms_state(): jnp.stack(frames, 0)]
  transfers between devices with their start and end apart: 2 -> 2, of which waited for: 2 -> 2; matrix products, arithmetic and copies ran while one was open for 6% -> 3% of each run, Pallas kernels for 0% -> 0%
where the time goes in v1:
time: 850 us; the launch traced here: 849 us
  waiting for transfers between devices  678 us (80%)
  local copies, waits for them, and re-layouts  64.9 us (8%)
  blocking collectives  41.8 us (5%)
  matrix products  31.9 us (4%)
  between operations  13.8 us (2%)
  other arithmetic  12 us (1%)
    all_to_all x1, waiting for transfers between devices, terms_state(): lax.all_to_all(jnp.stack(frames, 0), axis_name=a_name, split_axis=0, conc...  605 us
    reduce_scatter x1, waiting for transfers between devices, body(): lax.psum_scatter(partial_value.astype(jnp.bfloat16), 'tensor', scatter_di...  73.8 us
    all_to_all x1, blocking collectives, body(): lax.all_to_all(stacked, 'tensor', split_axis=1, concat_axis=0, tiled=True)  41.8 us
    gather x1, local copies, waits for them, and re-layouts, model_order(): return jnp.take(padded, source, axis=1)  23.8 us
    gather x1, local copies, waits for them, and re-layouts, padded_columns(): picked = jnp.take(matrix, source, axis=1)  18.3 us
  transfers between devices with their start and end apart: 2, of which 2 were waited for; matrix products, arithmetic and copies ran while one was open for 3% of the time, Pallas kernels for 0%

profile of v1, /device:TPU:0, one launch (start us, length us, event | category | flops | bytes accessed | tf_op | source)
XLA Modules:
  0.0 849.2 jit_solution(17218480037993770442)
XLA Ops:
  6.5 2.8 convert.33
  9.3 0.2 fusion.56
  9.5 0.7 copy.32
  10.2 0.1 slice.74
  10.3 0.6 copy.21
  10.9 0.7 copy.35
  11.6 0.1 slice.77
  11.7 0.6 copy.24
  12.5 0.2 pad_maximum_fusion
  12.7 41.8 %all_to_all.20 = bf16[68,8,2304]{2,0,1:T(8,128)(2,1)S(1)} all-to-all(bf16[68,8,2304]{2,0,1:T(8,128)(2,1)S(1)} %pad_maximum_fusion), channel_id=1, replica_groups=mesh['replica'=16,'tensor'=8] {'tensor'}, dimensions={1} | all-to-all | bytes 5013504 | tf_op jit(solution)/shard_map/all_to_all | solution.py:116
  54.5 2.1 stack_reshape.2
  56.7 14.3 %stack.3 = bf16[16,544,2304]{2,1,0:T(8,128)(2,1)} broadcast(bf16[544,2304]{1,0:T(8,128)(2,1)} %stack_reshape.2), dimensions={1,2} | broadcast | bytes 42614784 | tf_op jit(solution)/shard_map/stack | solution.py:127
  70.9 0.0 copy-start.1
  70.9 0.0 copy-start
  70.9 6.3 all-to-all-start.1
  77.3 0.0 copy-start.2
  77.3 0.0 reduce-scatter.2.cloned.1.call-start
  77.3 0.0 copy-done.1
  77.4 0.1 copy.19
  77.5 0.2 reduce-window.8
  77.6 0.1 reduce.4
  77.8 0.1 add_clamp_fusion
  77.9 0.1 min.18
  78.0 0.1 min.16
  78.1 0.0 copy-done
  78.1 0.1 reshape.406
  78.2 1.0 copy.20
  79.3 0.1 iota_compare_fusion.3
  79.3 0.1 lt.85
  79.5 0.0 copy-done.2
  79.5 0.1 add_convert_fusion.1
  79.5 0.1 convert_element_type.44
  79.6 0.1 fusion.36
  79.8 18.3 %gather_fusion = bf16[8704,16]{1,0:T(8,128)(2,1)} fusion(bf16[16,8192]{0,1:T(8,128)(2,1)S(1)} %copy.20, s32[9216]{0:T(1024)S(1)} %pad_clamp_fusion), kind=kCustom, calls=%fused_computation | custom fusion | bytes 591872 | tf_op jit(solution)/shard_map/jit(_take)/gather | solution.py:94
  98.0 0.1 multiply_cosine_fusion.1
  98.2 2.2 select_reduce_fusion
  100.4 0.1 compare_select_fusion.1
  100.5 0.1 iota_compare_fusion.2
  100.6 604.6 %all-to-all-done.1 = bf16[16,544,2304]{2,1,0:T(8,128)(2,1)} async-done(((bf16[16,544,2304]{2,1,0:T(8,128)(2,1)}), bf16[16,544,2304]{2,1,0:T(8,128)(2,1)}, u32[]{:S(2)}, u32[]{:S(2)}) %all-to-all-start.1) | async-done | bytes 40108064 | tf_op jit(solution)/shard_map/all_to_all | solution.py:127
  705.2 0.0 slice-start
  705.2 0.0 slice-start.1
  705.2 11.7 %fusion = f32[16,1280]{1,0:T(8,128)S(1)} fusion(bf16[8704,2304]{1,0:T(8,128)(2,1)} %bitcast.3, bf16[8704,16]{1,0:T(8,128)(2,1)} %gather_fusion, pred[8704]{0:T(1024)(128)(4,1)S(1)} %lt.85, pred[8704]{0:T(1024)(128)(4,1)S(1)} %compare_and_fusion), kind=kOutput, calls=%fused_computation.2 | convolution fusion | flops 356794368 | bytes 24609792 | tf_op jit(solution)/shard_map/dot_general | solution.py:132
  717.0 0.1 fusion.45
  717.1 0.1 subtract_convert_fusion
  717.2 0.0 slice-done
  717.2 0.0 slice-done.1
  717.2 2.4 fusion.58
  719.7 0.4 fusion.59
  720.1 0.4 fusion.25
  720.5 4.7 fusion.26
  725.2 0.2 fusion.29
  725.4 12.5 %fusion.2 = bf16[16,8704]{0,1:T(8,128)(2,1)} fusion(bf16[8704,2304]{1,0:T(8,128)(2,1)} %bitcast.3, bf16[2,8,8,128]{3,2,1,0:T(8,128)(2,1)S(1)} %bitcast.126), kind=kOutput, calls=%fused_computation.4 | convolution fusion | flops 285212672 | bytes 18137088 | tf_op jit(solution)/shard_map/tf,jf->tj/dot_general | solution.py:134
  738.0 23.8 %gather_fusion.1 = bf16[8192,16]{1,0:T(8,128)(2,1)S(1)} fusion(bf16[16,8704]{0,1:T(8,128)(2,1)} %fusion.2, s32[8192]{0:T(1024)S(1)} %broadcast_clamp_fusion), kind=kCustom, calls=%fused_computation.1 | custom fusion | bytes 557056 | tf_op jit(solution)/shard_map/jit(_take)/gather | solution.py:106
  761.8 5.0 fusion.24
  766.8 0.0 reduce-scatter.2.cloned.1.call-update
  766.9 73.8 %reduce-scatter.2.cloned.1.call-done = bf16[16,1024]{0,1:T(8,128)(2,1)} async-done(((bf16[16,8192]{0,1:T(8,128)(2,1)}), bf16[16,1024]{0,1:T(8,128)(2,1)}) %reduce-scatter.2.cloned.1.call-update) | async-done | bytes 32784 | tf_op jit(solution)/shard_map/reduce_scatter | solution.py:138
  840.6 1.0 copy.26
  841.7 0.6 reshape.420
  (23 shorter events, 0.3 us)
Async XLA Ops:
  70.9 6.4 copy-start.1
  70.9 7.2 copy-start
  70.9 634.3 %all-to-all-start.1 = ((bf16[16,544,2304]{2,1,0:T(8,128)(2,1)}), bf16[16,544,2304]{2,1,0:T(8,128)(2,1)}, u32[]{:S(2)}, u32[]{:S(2)}) async-start(bf16[16,544,2304]{2,1,0:T(8,128)(2,1)} %stack.3), calls=%async_computation.1 | async-start | bytes 80216064 | tf_op jit(solution)/shard_map/all_to_all | solution.py:127
  77.3 2.2 copy-start.2
  77.3 763.3 %reduce-scatter.2.cloned.1.call-start = ((), (), s32[]{:S(2)}) async-start(), calls=%async_computation.3 | async-start | bytes 2359296 | tf_op jit(solution)/shard_map/reduce_scatter | solution.py:138
  705.2 12.0 %slice-start = ((s8[8388608]{0:T(1024)(128)(4,1)}), s8[4194304]{0:T(1024)(128)(4,1)S(1)}, s32[]{:S(2)}) async-start(s8[8388608]{0:T(1024)(128)(4,1)} %bitcast.104), calls=%async_computation.4 | async-start | bytes 8388608
  705.2 12.0 %slice-start.1 = ((s8[8388608]{0:T(1024)(128)(4,1)}), s8[4194304]{0:T(1024)(128)(4,1)S(1)}, s32[]{:S(2)}) async-start(s8[8388608]{0:T(1024)(128)(4,1)} %bitcast.104), calls=%async_computation.5 | async-start | bytes 8388608
Sparse Core Ops, SparseCore 0:
  767.0 73.6 reduce-scatter.1
